TPU v7x, 32 devices: a whole 2x2x4 slice. The times are simulated.
32 devices in a mesh: space: 2 (over x), vel: 16 (over z, y, core).
Axes of the slice: x: 2, y: 2, z: 4, core: 2. Of those that a mesh axis runs over, the one named last changes fastest.
Arguments:
- distribution: float32 [8192, 512], P('vel', 'space'), may hold values from 0.1 to 32, as said below
- normals: float32 [4, 3, 512], P(None, None, 'space'), may hold values from -0.3 to 0.3
- adjacency: int32 [4, 512], P(None, 'space'), may hold values from 0 to 511, as said below
- send_list: int32 [2, 2, 256], P('space'), may hold values from 0 to 255
- block_counts: int32 [2, 2], P(None, 'space'), may hold values from 0 to 2, as said below
Outputs:
- relaxed: float32 [8192, 512], P('vel', 'space')
- fields: float32 [13, 512], P(None, 'space')
Inputs may be any that keep to these rules, and one draw needn't show every extreme that they name: `adjacency`: every entry of 256 or more names a position below 128 times the sum of block_counts over the senders to its group. `block_counts`: no group sends to itself; every other pair has at least one block; one receiving group gets 2 blocks from every other group. `distribution`: Positive.
All inputs are finite; a program needn't handle non-finite values.
Results may differ from a plain program's by a relative error of at most 0.00011.
Values sent between devices are 32-bit elements; how exact they have to be, the bound alone decides.
A program may use at most 64 MiB of HBM per device.

v0:
```python
import jax
import jax.numpy as jnp
from jax import lax
from jax.sharding import PartitionSpec as P

VXY = 32
TILE = 128
ITERS = 2
spacing = 0.3
ellipsoid_mix = -0.25
prandtl = 0.8
visc_power = 0.26
time_step = 0.025


def velocity_nodes(vel_index, z_count):
    comp_x = (vel_index % VXY).astype(jnp.float32)
    comp_y = (vel_index // VXY % VXY).astype(jnp.float32)
    comp_z = (vel_index // (VXY * VXY)).astype(jnp.float32)
    centre = (VXY - 1) / 2.0
    return jnp.stack(
        [
            (comp_x - centre) * spacing,
            (comp_y - centre) * spacing,
            (comp_z - (z_count - 1) / 2.0) * spacing,
        ]
    )


def moment_rows(velocity):
    comp_x, comp_y, comp_z = (velocity[0], velocity[1], velocity[2])
    squared = comp_x * comp_x + comp_y * comp_y + comp_z * comp_z
    return jnp.stack(
        [
            jnp.ones_like(comp_x),
            comp_x,
            comp_y,
            comp_z,
            comp_x * comp_x,
            comp_y * comp_y,
            comp_z * comp_z,
            comp_x * comp_y,
            comp_x * comp_z,
            comp_y * comp_z,
            comp_x * squared,
            comp_y * squared,
            comp_z * squared,
        ]
    )


def quad_rows(velocity):
    comp_x, comp_y, comp_z = (velocity[0], velocity[1], velocity[2])
    return jnp.stack(
        [
            comp_x * comp_x,
            comp_y * comp_y,
            comp_z * comp_z,
            comp_x * comp_y,
            comp_x * comp_z,
            comp_y * comp_z,
            comp_x,
            comp_y,
            comp_z,
            jnp.ones_like(comp_x),
        ]
    )


def macroscopic(moments):
    density = moments[0]
    mean_x = moments[1] / density
    mean_y = moments[2] / density
    mean_z = moments[3] / density
    second = moments[4:10] / density[None, :]
    third = moments[10:13] / density[None, :]
    theta_xx = second[0] - mean_x * mean_x
    theta_yy = second[1] - mean_y * mean_y
    theta_zz = second[2] - mean_z * mean_z
    theta_xy = second[3] - mean_x * mean_y
    theta_xz = second[4] - mean_x * mean_z
    theta_yz = second[5] - mean_y * mean_z
    temper = (theta_xx + theta_yy + theta_zz) / 3.0
    trace_b = second[0] + second[1] + second[2]
    bu_x = second[0] * mean_x + second[3] * mean_y + second[4] * mean_z
    bu_y = second[3] * mean_x + second[1] * mean_y + second[5] * mean_z
    bu_z = second[4] * mean_x + second[5] * mean_y + second[2] * mean_z
    mean_sq = mean_x * mean_x + mean_y * mean_y + mean_z * mean_z
    flux_x = 0.5 * (third[0] - 2.0 * bu_x - mean_x * trace_b + 2.0 * mean_x * mean_sq)
    flux_y = 0.5 * (third[1] - 2.0 * bu_y - mean_y * trace_b + 2.0 * mean_y * mean_sq)
    flux_z = 0.5 * (third[2] - 2.0 * bu_z - mean_z * trace_b + 2.0 * mean_z * mean_sq)
    iso_part = (1.0 - ellipsoid_mix) * temper
    lam_xx = iso_part + ellipsoid_mix * theta_xx
    lam_yy = iso_part + ellipsoid_mix * theta_yy
    lam_zz = iso_part + ellipsoid_mix * theta_zz
    lam_xy = ellipsoid_mix * theta_xy
    lam_xz = ellipsoid_mix * theta_xz
    lam_yz = ellipsoid_mix * theta_yz
    cof_xx = lam_yy * lam_zz - lam_yz * lam_yz
    cof_xy = lam_yz * lam_xz - lam_xy * lam_zz
    cof_xz = lam_xy * lam_yz - lam_yy * lam_xz
    cof_yy = lam_xx * lam_zz - lam_xz * lam_xz
    cof_yz = lam_xy * lam_xz - lam_xx * lam_yz
    cof_zz = lam_xx * lam_yy - lam_xy * lam_xy
    determinant = lam_xx * cof_xx + lam_xy * cof_xy + lam_xz * cof_xz
    inv_xx = cof_xx / determinant
    inv_yy = cof_yy / determinant
    inv_zz = cof_zz / determinant
    inv_xy = cof_xy / determinant
    inv_xz = cof_xz / determinant
    inv_yz = cof_yz / determinant
    lin_x = inv_xx * mean_x + inv_xy * mean_y + inv_xz * mean_z
    lin_y = inv_xy * mean_x + inv_yy * mean_y + inv_yz * mean_z
    lin_z = inv_xz * mean_x + inv_yz * mean_y + inv_zz * mean_z
    offset = mean_x * lin_x + mean_y * lin_y + mean_z * lin_z
    collide = prandtl * density * jnp.exp(visc_power * jnp.log(temper))
    return jnp.stack(
        [
            density,
            mean_x,
            mean_y,
            mean_z,
            theta_xx,
            theta_yy,
            theta_zz,
            theta_xy,
            theta_xz,
            theta_yz,
            flux_x,
            flux_y,
            flux_z,
            inv_xx,
            inv_yy,
            inv_zz,
            2.0 * inv_xy,
            2.0 * inv_xz,
            2.0 * inv_yz,
            -2.0 * lin_x,
            -2.0 * lin_y,
            -2.0 * lin_z,
            offset,
            collide,
        ]
    )


def ghost_slots(adjacency, counts, cells, groups, slot_count):
    ends = jnp.cumsum(counts) * TILE
    starts = ends - counts * TILE
    is_local = adjacency < cells
    position = jnp.maximum(adjacency - cells, 0)
    source = jnp.sum((ends[:, None, None] <= position[None]).astype(jnp.int32), axis=0)
    source = jnp.minimum(source, groups - 1)
    group_ids = jnp.arange(groups, dtype=jnp.int32)[:, None, None]
    chosen = jnp.sum(jnp.where(group_ids == source[None], starts[:, None, None], 0), axis=0)
    slot_pos = jnp.clip(position - chosen, 0, slot_count - 1)
    return (is_local, source, slot_pos)


def relax(current, neighbours, velocity, normals, params, norm_z, equilibrium):
    gauss = params[0][None, :] * equilibrium / norm_z[None, :]
    outflow = jnp.zeros(current.shape, jnp.float32)
    inflow = jnp.zeros(current.shape, jnp.float32)
    for side in range(normals.shape[0]):
        normal_speed = (
            velocity[0][:, None] * normals[side, 0][None, :]
            + velocity[1][:, None] * normals[side, 1][None, :]
            + velocity[2][:, None] * normals[side, 2][None, :]
        )
        outflow = outflow + jnp.maximum(normal_speed, 0.0)
        inflow = inflow + jnp.minimum(normal_speed, 0.0) * neighbours[side]
    return current + time_step * (
        params[23][None, :] * (gauss - current) - outflow * current - inflow
    )


def per_device(distribution, normals, adjacency, send_list, block_counts):
    vel_local = distribution.shape[0]
    cells = distribution.shape[1]
    total_vel = vel_local * lax.axis_size("vel")
    z_count = total_vel // (VXY * VXY)
    groups = send_list.shape[1]
    slot_count = send_list.shape[2]
    vel_index = lax.axis_index("vel") * vel_local + jnp.arange(vel_local, dtype=jnp.int32)
    velocity = velocity_nodes(vel_index, z_count)
    moment_table = moment_rows(velocity)
    quad_table = quad_rows(velocity).T
    is_local, source, slot_pos = ghost_slots(
        adjacency, block_counts[:, 0], cells, groups, slot_count
    )
    ghost_index = source * slot_count + slot_pos
    local_index = jnp.where(is_local, adjacency, 0)
    send_rows = send_list[0].reshape(-1)

    def reduce_moments(current):
        partial_value = (
            jnp.dot(
                moment_table,
                current,
                precision=lax.Precision.HIGHEST,
                preferred_element_type=jnp.float32,
            )
            / total_vel
        )
        return macroscopic(lax.psum(partial_value, "vel"))

    current = distribution
    for iteration in range(ITERS):
        params = reduce_moments(current)
        ghosts = lax.all_to_all(
            jnp.take(current, send_rows, axis=1), "space", split_axis=1, concat_axis=1, tiled=True
        )
        exponent = jnp.dot(
            quad_table,
            params[13:23],
            precision=lax.Precision.HIGHEST,
            preferred_element_type=jnp.float32,
        )
        equilibrium = jnp.exp(-0.5 * exponent)
        norm_z = lax.psum(jnp.sum(equilibrium, axis=0) / total_vel, "vel")
        neighbours = [
            jnp.where(
                is_local[side][None, :],
                jnp.take(current, local_index[side], axis=1),
                jnp.take(ghosts, ghost_index[side], axis=1),
            )
            for side in range(normals.shape[0])
        ]
        current = relax(current, neighbours, velocity, normals, params, norm_z, equilibrium)
    final = reduce_moments(current)
    return (current, final[:13])


def solution(mesh):
    placed = (
        P("vel", "space"),
        P(None, None, "space"),
        P(None, "space"),
        P("space", None, None),
        P(None, "space"),
    )
    return jax.shard_map(
        per_device,
        mesh=mesh,
        in_specs=placed,
        out_specs=(P("vel", "space"), P(None, "space")),
        check_vma=False,
    )
```

profile of v0, /device:TPU:0, one launch (start us, length us, event | category | flops | bytes accessed | tf_op | source)
XLA Modules:
  0.0 309.6 jit_solution(3086310342836148335)
XLA Ops:
  5.4 4.4 %all-to-all-start = ((f32[512,2,256]{0,2,1:T(8,128)}), f32[512,2,256]{0,2,1:T(8,128)S(1)}, u32[]{:S(2)}, u32[]{:S(2)}) async-start(f32[512,2,256]{0,2,1:T(8,128)} %bitcast.20), calls=%async_computation | async-start | bytes 2097152 | tf_op jit(solution)/shard_map/all_to_all | solution.py:210
  11.7 62.4 %psum.35 = f32[13,256]{1,0:T(8,128)S(1)} all-reduce(f32[13,256]{1,0:T(8,128)S(1)} %convolution_multiply_fusion.4), channel_id=1, replica_groups=mesh['space'=2,'vel'=16] {'vel'}, use_global_device_ids=true, to_apply=%region_0.1 | all-reduce | flops 3328 | bytes 26624 | tf_op jit(solution)/shard_map/psum | solution.py:205
  74.9 29.5 %psum.36 = f32[256]{0:T(256)S(1)} all-reduce(f32[256]{0:T(256)S(1)} %broadcast_multiply_fusion.1), channel_id=1, replica_groups=mesh['space'=2,'vel'=16] {'vel'}, use_global_device_ids=true, to_apply=%region_2.3 | all-reduce | flops 256 | bytes 2048 | tf_op jit(solution)/shard_map/psum | solution.py:220
  104.5 1.8 gather_fusion
  107.5 1.8 gather_fusion.3
  109.3 2.0 copy.38
  111.3 1.8 gather_fusion.5
  113.1 2.1 copy.41
  115.1 1.8 gather_fusion.7
  116.9 2.1 copy.44
  125.0 1.8 gather_fusion.8
  126.7 2.1 copy.45
  128.9 2.9 fusion.16
  132.3 57.6 %psum.37 = f32[13,256]{1,0:T(8,128)S(1)} all-reduce(f32[13,256]{1,0:T(8,128)S(1)} %convolution_multiply_fusion.3), channel_id=1, replica_groups=mesh['space'=2,'vel'=16] {'vel'}, use_global_device_ids=true, to_apply=%region_6.10 | all-reduce | flops 3328 | bytes 26624 | tf_op jit(solution)/shard_map/psum | solution.py:205
  192.9 3.8 %all-to-all-start.1 = ((f32[512,2,256]{0,2,1:T(8,128)}), f32[512,2,256]{0,2,1:T(8,128)S(1)}, u32[]{:S(2)}, u32[]{:S(2)}) async-start(f32[512,2,256]{0,2,1:T(8,128)} %bitcast.39), calls=%async_computation.1 | async-start | bytes 2097152 | tf_op jit(solution)/shard_map/all_to_all | solution.py:210
  198.6 1.8 gather_fusion.14
  200.4 1.8 gather_fusion.16
  202.6 2.1 copy.54
  207.2 29.5 %psum.38 = f32[256]{0:T(256)S(1)} all-reduce(f32[256]{0:T(256)S(1)} %broadcast_multiply_fusion), channel_id=1, replica_groups=mesh['space'=2,'vel'=16] {'vel'}, use_global_device_ids=true, to_apply=%region_8.12 | all-reduce | flops 256 | bytes 2048 | tf_op jit(solution)/shard_map/psum | solution.py:220
  237.6 1.8 gather_fusion.13
  239.4 1.8 gather_fusion.15
  241.2 1.8 gather_fusion.17
  247.4 2.9 fusion.6
  250.7 57.7 %psum.39 = f32[13,256]{1,0:T(8,128)S(1)} all-reduce(f32[13,256]{1,0:T(8,128)S(1)} %convolution_multiply_fusion.2), channel_id=1, replica_groups=mesh['space'=2,'vel'=16] {'vel'}, use_global_device_ids=true, to_apply=%region_9.13 | all-reduce | flops 3328 | bytes 26624 | tf_op jit(solution)/shard_map/psum | solution.py:205
  (139 shorter events, 29.9 us)
Async XLA Ops:
  5.3 6.0 %copy-start = (f32[512,256]{1,0:T(8,128)S(1)}, f32[512,256]{1,0:T(8,128)}, u32[]{:S(2)}) copy-start(f32[512,256]{1,0:T(8,128)} %param.11) | copy-start | bytes 1572868
  5.4 113.7 %all-to-all-start = ((f32[512,2,256]{0,2,1:T(8,128)}), f32[512,2,256]{0,2,1:T(8,128)S(1)}, u32[]{:S(2)}, u32[]{:S(2)}) async-start(f32[512,2,256]{0,2,1:T(8,128)} %bitcast.20), calls=%async_computation | async-start | bytes 2097152 | tf_op jit(solution)/shard_map/all_to_all | solution.py:210
  10.0 0.7 copy-start.12
  10.0 0.8 copy-start.10
  116.9 2.1 copy-start.11
  126.7 2.1 copy-start.4
  126.7 2.1 copy-start.5
  192.9 43.8 %all-to-all-start.1 = ((f32[512,2,256]{0,2,1:T(8,128)}), f32[512,2,256]{0,2,1:T(8,128)S(1)}, u32[]{:S(2)}, u32[]{:S(2)}) async-start(f32[512,2,256]{0,2,1:T(8,128)} %bitcast.39), calls=%async_computation.1 | async-start | bytes 2097152 | tf_op jit(solution)/shard_map/all_to_all | solution.py:210
  202.5 2.1 copy-start.6
  242.9 1.0 copy-start.7
  244.0 1.0 copy-start.8
  245.0 1.0 copy-start.9
  246.1 1.0 copy-start.2
  246.1 1.4 copy-start.3
  250.4 59.3 %copy-start.1 = (f32[512,256]{1,0:T(8,128)}, f32[512,256]{1,0:T(8,128)S(1)}, u32[]{:S(2)}) copy-start(f32[512,256]{1,0:T(8,128)S(1)} %fusion.6) | copy-start | bytes 1572868
where the time goes:
time: 311 us; the launch traced here: 310 us
  blocking collectives  237 us (76%)
  local copies, waits for them, and re-layouts  51.6 us (17%)
  other arithmetic  9.24 us (3%)
  starting transfers between devices  8.12 us (3%)
    psum x3, blocking collectives, reduce_moments(): return macroscopic(lax.psum(partial_value, 'vel'))  178 us
    psum x2, blocking collectives, per_device(): norm_z = lax.psum(jnp.sum(equilibrium, axis=0) / total_vel, 'vel')  59 us
    gather x16, local copies, waits for them, and re-layouts, per_device(): jnp.take(current, local_index[side], axis=1)  23.4 us
    gather x16, local copies, waits for them, and re-layouts, per_device(): jnp.take(ghosts, ghost_index[side], axis=1)  20.1 us
    all_to_all x2, starting transfers between devices, per_device(): lax.all_to_all(jnp.take(current, send_rows, axis=1), 'space', split_axis=...  8.12 us
  transfers between devices with their start and end apart: 2, of which 0 were waited for; matrix products, arithmetic and copies ran while one was open for 9% of the time, Pallas kernels for 0%

commit v1 on v0

--- a/solution.py
+++ b/solution.py
@@ -217,7 +217,9 @@
             preferred_element_type=jnp.float32,
         )
         equilibrium = jnp.exp(-0.5 * exponent)
-        norm_z = lax.psum(jnp.sum(equilibrium, axis=0) / total_vel, "vel")
+        part = jnp.sum(equilibrium, axis=0) / total_vel
+        parts = lax.all_gather(part, "vel")
+        norm_z = jnp.sum(parts, axis=0)
         neighbours = [
             jnp.where(
                 is_local[side][None, :],

time: 311 us -> 294 us (0.945)
  blocking collectives: 237 us -> 216 us
  local copies, waits for them, and re-layouts: 51.6 us -> 56.3 us
    psum x2 -> x0, blocking collectives: 59 us -> none  [per_device(): norm_z = lax.psum(jnp.sum(equilibrium, axis=0) / total_vel, 'vel')]
    all_gather x0 -> x2, blocking collectives: none -> 34.3 us  [per_device(): parts = lax.all_gather(part, 'vel')]
    psum x3, blocking collectives: 178 us -> 181 us  [reduce_moments(): return macroscopic(lax.psum(partial_value, 'vel'))]
    gather x16, local copies, waits for them, and re-layouts: 23.4 us -> 26.8 us  [per_device(): jnp.take(current, local_index[side], axis=1)]
  transfers between devices with their start and end apart: 2 -> 2, of which waited for: 0 -> 0; matrix products, arithmetic and copies ran while one was open for 9% -> 10% of each run, Pallas kernels for 0% -> 0%
where the time goes in v1:
time: 294 us; the launch traced here: 293 us
  blocking collectives  216 us (73%)
  local copies, waits for them, and re-layouts  56.3 us (19%)
  other arithmetic  9.31 us (3%)
  starting transfers between devices  8.12 us (3%)
    psum x3, blocking collectives, reduce_moments(): return macroscopic(lax.psum(partial_value, 'vel'))  181 us
    all_gather x2, blocking collectives, per_device(): parts = lax.all_gather(part, 'vel')  34.3 us
    gather x16, local copies, waits for them, and re-layouts, per_device(): jnp.take(current, local_index[side], axis=1)  26.8 us
    gather x16, local copies, waits for them, and re-layouts, per_device(): jnp.take(ghosts, ghost_index[side], axis=1)  21.2 us
    all_to_all x2, starting transfers between devices, per_device(): lax.all_to_all(jnp.take(current, send_rows, axis=1), 'space', split_axis=...  8.12 us
  transfers between devices with their start and end apart: 2, of which 0 were waited for; matrix products, arithmetic and copies ran while one was open for 10% of the time, Pallas kernels for 0%

profile of v1, /device:TPU:0, one launch (start us, length us, event | category | flops | bytes accessed | tf_op | source)
XLA Modules:
  0.0 292.7 jit_solution(5374716571696782291)
XLA Ops:
  5.4 4.4 %all-to-all-start = ((f32[512,2,256]{0,2,1:T(8,128)}), f32[512,2,256]{0,2,1:T(8,128)S(1)}, u32[]{:S(2)}, u32[]{:S(2)}) async-start(f32[512,2,256]{0,2,1:T(8,128)} %bitcast.21), calls=%async_computation | async-start | bytes 2097152 | tf_op jit(solution)/shard_map/all_to_all | solution.py:210
  11.7 62.4 %psum.21 = f32[13,256]{1,0:T(8,128)S(1)} all-reduce(f32[13,256]{1,0:T(8,128)S(1)} %convolution_multiply_fusion.4), channel_id=1, replica_groups=mesh['space'=2,'vel'=16] {'vel'}, use_global_device_ids=true, to_apply=%region_0.1 | all-reduce | flops 3328 | bytes 26624 | tf_op jit(solution)/shard_map/psum | solution.py:205
  74.9 17.2 %all-gather.2 = f32[16,1,256]{2,1,0:T(1,128)S(1)} all-gather(f32[1,1,256]{2,1,0:T(1,128)S(1)} %bitcast.195), channel_id=2, replica_groups=mesh['space'=2,'vel'=16] {'vel'}, dimensions={0}, use_global_device_ids=true | all-gather | bytes 17408 | tf_op jit(solution)/shard_map/all_gather | solution.py:221
  92.2 1.8 gather_fusion
  95.2 1.8 gather_fusion.3
  96.9 2.0 copy.64
  99.0 1.8 gather_fusion.5
  100.7 2.1 copy.67
  104.6 2.1 copy.70
  115.1 2.1 copy.71
  117.2 2.9 %fusion.16 = f32[512,256]{1,0:T(8,128)S(1)} fusion(f32[512,256]{1,0:T(8,128)S(1)} %copy-done, f32[256,512]{0,1:T(8,128)} %copy.71, f32[256,512]{0,1:T(8,128)} %copy.70, f32[256,512]{0,1:T(8,128)} %copy.68, f32[256,512]{0,1:T(8,128)S(1)} %copy-done.5, f32[256,512]{0,1:T(8,128)} %copy.65, f32[256,512]{0,1:T(8,128)S(1)} %copy-done.2, f32[256,512]{0,1:T(8,128)} %copy.62, ...), kind=kLoop, calls=%fused_computation.44 | loop fusion | flops 7733248 | bytes 5791744 | tf_op jit(solution)/shard_map/add | solution.py:172
  120.7 59.4 %psum.22 = f32[13,256]{1,0:T(8,128)S(1)} all-reduce(f32[13,256]{1,0:T(8,128)S(1)} %convolution_multiply_fusion.3), channel_id=1, replica_groups=mesh['space'=2,'vel'=16] {'vel'}, use_global_device_ids=true, to_apply=%region_6.10 | all-reduce | flops 3328 | bytes 26624 | tf_op jit(solution)/shard_map/psum | solution.py:205
  183.0 3.8 %all-to-all-start.1 = ((f32[512,2,256]{0,2,1:T(8,128)}), f32[512,2,256]{0,2,1:T(8,128)S(1)}, u32[]{:S(2)}, u32[]{:S(2)}) async-start(f32[512,2,256]{0,2,1:T(8,128)} %bitcast.41), calls=%async_computation.1 | async-start | bytes 2097152 | tf_op jit(solution)/shard_map/all_to_all | solution.py:210
  186.8 1.8 gather_fusion.9
  188.6 1.8 gather_fusion.12
  190.3 1.8 gather_fusion.14
  194.6 17.2 %all-gather.3 = f32[16,1,256]{2,1,0:T(1,128)S(1)} all-gather(f32[1,1,256]{2,1,0:T(1,128)S(1)} %bitcast.196), channel_id=3, replica_groups=mesh['space'=2,'vel'=16] {'vel'}, dimensions={0}, use_global_device_ids=true | all-gather | bytes 17408 | tf_op jit(solution)/shard_map/all_gather | solution.py:221
  212.0 2.1 copy.77
  215.1 2.1 copy.83
  218.2 1.8 gather_fusion.13
  219.9 1.8 gather_fusion.15
  226.5 2.1 copy.84
  228.7 2.9 %fusion.6 = f32[512,256]{1,0:T(8,128)S(1)} fusion(f32[512,256]{1,0:T(8,128)S(1)} %fusion.16, f32[256,512]{0,1:T(8,128)} %copy.84, f32[256,512]{0,1:T(8,128)} %copy.83, f32[256,512]{0,1:T(8,128)} %copy.81, f32[256,512]{0,1:T(8,128)S(1)} %copy-done.4, f32[256,512]{0,1:T(8,128)} %copy.78, f32[256,512]{0,1:T(8,128)S(1)} %copy-done.3, f32[256,512]{0,1:T(8,128)} %copy.75, ...), kind=kLoop, calls=%fused_computation.30 | loop fusion | flops 7733248 | bytes 5791744 | tf_op jit(solution)/shard_map/add | solution.py:172
  231.9 59.5 %psum.23 = f32[13,256]{1,0:T(8,128)S(1)} all-reduce(f32[13,256]{1,0:T(8,128)S(1)} %convolution_multiply_fusion.2), channel_id=1, replica_groups=mesh['space'=2,'vel'=16] {'vel'}, use_global_device_ids=true, to_apply=%region_9.13 | all-reduce | flops 3328 | bytes 26624 | tf_op jit(solution)/shard_map/psum | solution.py:205
  (141 shorter events, 33.2 us)
Async XLA Ops:
  5.3 6.0 %copy-start = (f32[512,256]{1,0:T(8,128)S(1)}, f32[512,256]{1,0:T(8,128)}, u32[]{:S(2)}) copy-start(f32[512,256]{1,0:T(8,128)} %param.11) | copy-start | bytes 1572868
  5.4 102.0 %all-to-all-start = ((f32[512,2,256]{0,2,1:T(8,128)}), f32[512,2,256]{0,2,1:T(8,128)S(1)}, u32[]{:S(2)}, u32[]{:S(2)}) async-start(f32[512,2,256]{0,2,1:T(8,128)} %bitcast.21), calls=%async_computation | async-start | bytes 2097152 | tf_op jit(solution)/shard_map/all_to_all | solution.py:210
  10.0 0.7 copy-start.12
  10.0 0.8 copy-start.10
  106.6 0.7 copy-start.11
  115.1 2.1 copy-start.2
  115.1 2.1 copy-start.5
  183.0 34.2 %all-to-all-start.1 = ((f32[512,2,256]{0,2,1:T(8,128)}), f32[512,2,256]{0,2,1:T(8,128)S(1)}, u32[]{:S(2)}, u32[]{:S(2)}) async-start(f32[512,2,256]{0,2,1:T(8,128)} %bitcast.41), calls=%async_computation.1 | async-start | bytes 2097152 | tf_op jit(solution)/shard_map/all_to_all | solution.py:210
  193.9 17.9 %copy-start.6 = (f32[256,512]{1,0:T(8,128)S(1)}, f32[256,512]{1,0:T(8,128)}, u32[]{:S(2)}) copy-start(f32[256,512]{1,0:T(8,128)} %gather_fusion.9) | copy-start | bytes 1572868
  212.0 2.1 copy-start.7
  223.5 1.0 copy-start.8
  224.5 1.0 copy-start.9
  226.5 2.1 copy-start.3
  226.5 2.1 copy-start.4
  231.6 61.1 %copy-start.1 = (f32[512,256]{1,0:T(8,128)}, f32[512,256]{1,0:T(8,128)S(1)}, u32[]{:S(2)}) copy-start(f32[512,256]{1,0:T(8,128)S(1)} %fusion.6) | copy-start | bytes 1572868
